TPU v7x, 256 devices: a whole 4x4x8 slice. The times are simulated.
256 devices in a mesh: dp: 8 (over x, y_hi), seq: 32 (over y_lo, z, core).
Axes of the slice: x: 4, y: 4 (y_hi: 2, y_lo: 2; y = y_hi * 2 + y_lo), z: 8, core: 2. Of those that a mesh axis runs over, the one named last changes fastest.
Arguments:
- inputs: bfloat16 [8, 16384, 1024], P('dp', 'seq'), may hold values from -6 to 6
- out_grad: bfloat16 [8, 16384, 1024], P('dp', 'seq'), may hold values from -6 to 6
- w_in: bfloat16 [1024, 3072], replicated, may hold values from -0.1875 to 0.1875
- taps: float32 [3, 3072], replicated, may hold values from -3 to 3
- filt: bfloat16 [64, 256, 1024], P(None, 'seq'), may hold values from -4 to 4
Outputs:
- mixed: bfloat16 [8, 16384, 1024], P('dp', 'seq')
- in_grad: bfloat16 [8, 16384, 1024], P('dp', 'seq')
- w_in_grad: float32 [1024, 3072], P('dp', 'seq')
- taps_grad: float32 [3, 3072], replicated
All inputs are finite; a program needn't handle non-finite values.
Results may differ from a plain program's by a relative error of at most 0.012.
Values may be sent and summed in bfloat16 or wider, within the bound.
A program may use at most 128 MiB of HBM per device.

v0:
```python
import math
import jax
import jax.numpy as jnp
from jax import lax
from jax.sharding import PartitionSpec as P

BLK = 256


def padded(cells, sides, width):
    for axis, dim in sides:
        count = lax.axis_size(axis)
        ends = count - 1
        head = lax.slice_in_dim(cells, 0, width, axis=dim)
        tail = lax.slice_in_dim(cells, cells.shape[dim] - width, cells.shape[dim], axis=dim)
        cells = jnp.concatenate(
            [
                lax.ppermute(tail, axis, [(i, (i + 1) % count) for i in range(ends)]),
                cells,
                lax.ppermute(head, axis, [((i + 1) % count, i) for i in range(ends)]),
            ],
            axis=dim,
        )
    return cells


def dct_table(count):
    rows = jnp.arange(count, dtype=jnp.float32)[:, None]
    cols = jnp.arange(count, dtype=jnp.float32)[None, :]
    first = jnp.where(rows == 0, jnp.float32(math.sqrt(0.5)), jnp.float32(1.0))
    table = (
        jnp.float32(math.sqrt(2.0 / count))
        * first
        * jnp.cos(jnp.float32(math.pi) * (cols + 0.5) * rows / count)
    )
    return table.astype(jnp.bfloat16)


def block_section(blocks, table_q):
    return jnp.einsum("rq,nbqd->nbrd", table_q, blocks, preferred_element_type=jnp.float32).astype(
        jnp.bfloat16
    )


def span_section(columns, filt, table_p):
    stack, span, narrow, width = columns.shape
    flat = columns.reshape(stack, span, narrow * width)
    second = jnp.einsum("ap,npk->nak", table_p, flat, preferred_element_type=jnp.float32)
    scaled = (filt.reshape(1, span, narrow * width).astype(jnp.float32) * second).astype(
        jnp.bfloat16
    )
    third = jnp.einsum("ap,nak->npk", table_p, scaled, preferred_element_type=jnp.float32).astype(
        jnp.bfloat16
    )
    return third.reshape(columns.shape)


def final_section(blocks, table_q):
    return jnp.einsum("rq,nbrd->nbqd", table_q, blocks, preferred_element_type=jnp.float32)


def shards(inputs, out_grad, w_in, taps, filt):
    tok = inputs.shape[1]
    width = inputs.shape[2]
    nseq = lax.axis_size("seq")
    ndata = lax.axis_size("dp")
    nblocks = tok // BLK
    table_q = dct_table(BLK)
    table_p = dct_table(filt.shape[0])
    factor = 1.0 / math.sqrt(ndata * nseq * tok)
    rows = inputs[0]
    z = jnp.dot(rows, w_in, preferred_element_type=jnp.float32).astype(jnp.bfloat16)
    zpad = padded(z, (("seq", 0),), 1)
    s = taps[0] * zpad[:-2] + taps[1] * zpad[1:-1] + taps[2] * zpad[2:]
    a_part = s[:, :width]
    g_part = s[:, width : 2 * width]
    v_part = s[:, 2 * width :]
    w = (a_part * v_part).astype(jnp.bfloat16)
    gradf = out_grad[0].astype(jnp.float32)
    e4 = (gradf * g_part).astype(jnp.bfloat16)
    columns = lax.all_to_all(
        block_section(w.reshape(1, nblocks, BLK, width), table_q),
        "seq",
        split_axis=2,
        concat_axis=1,
        tiled=True,
    )
    back = lax.all_to_all(
        span_section(columns, filt, table_p), "seq", split_axis=1, concat_axis=2, tiled=True
    )
    h4 = final_section(back, table_q).reshape(tok, width)
    grad_cols = lax.all_to_all(
        block_section(e4.reshape(1, nblocks, BLK, width), table_q),
        "seq",
        split_axis=2,
        concat_axis=1,
        tiled=True,
    )
    grad_back = lax.all_to_all(
        span_section(grad_cols, filt, table_p), "seq", split_axis=1, concat_axis=2, tiled=True
    )
    dw = final_section(grad_back, table_q).reshape(tok, width)
    mixed = (g_part * h4).astype(jnp.bfloat16)
    ds = jnp.concatenate([dw * v_part, gradf * h4, dw * a_part], axis=1).astype(jnp.bfloat16)
    dspad = padded(ds, (("seq", 0),), 1)
    du = (taps[0] * dspad[2:] + taps[1] * dspad[1:-1] + taps[2] * dspad[:-2]).astype(jnp.bfloat16)
    in_grad = jnp.dot(du, w_in.T, preferred_element_type=jnp.float32).astype(jnp.bfloat16)
    dsf = ds.astype(jnp.float32)
    zf = zpad.astype(jnp.float32)
    local_taps = jnp.stack([jnp.sum(dsf * zf[k : k + tok], axis=0) for k in range(3)])
    taps_grad = lax.psum(local_taps, ("dp", "seq")) * factor
    contract = (((0,), (0,)), ((), ()))
    partial_sum = lax.psum_scatter(
        lax.dot_general(rows, du, contract, preferred_element_type=jnp.float32),
        "dp",
        scatter_dimension=0,
        tiled=True,
    )
    w_grad = lax.psum_scatter(partial_sum, "seq", scatter_dimension=1, tiled=True) * factor
    return (mixed[None], in_grad[None], w_grad, taps_grad)


def solution(mesh):
    return jax.shard_map(
        shards,
        mesh=mesh,
        in_specs=(P("dp", "seq", None), P("dp", "seq", None), P(), P(), P(None, "seq", None)),
        out_specs=(P("dp", "seq", None), P("dp", "seq", None), P("dp", "seq"), P()),
        check_vma=False,
    )
```

profile of v0, /device:TPU:2, one launch (start us, length us, event | category | flops | bytes accessed | tf_op | source)
XLA Modules:
  0.0 500.8 jit_solution(6452901341456452620)
XLA Ops:
  8.4 6.4 %convolution_convert_fusion.2 = bf16[512,3072]{1,0:T(8,128)(2,1)S(1)} fusion(bf16[1024,3072]{1,0:T(8,128)(2,1)} %param.7, bf16[1,512,1024]{2,1,0:T(8,128)(2,1)S(1)} %copy-done), kind=kOutput, calls=%fused_computation.22 | convolution fusion | flops 3222798336 | bytes 10485760 | tf_op jit(solution)/shard_map/dot_general | solution.py:72
  14.9 2.0 collective-permute-start
  18.2 3.4 collective-permute-done.1
  21.6 2.5 multiply_add_fusion
  24.2 2.7 copy-done.2
  27.2 1.4 fusion.19
  28.6 2.1 copy.34
  30.7 11.8 %all-to-all-start.2 = ((bf16[1,2,256,1024]{3,1,0,2:T(2,128)(2,1)}), bf16[1,2,256,1024]{3,1,0,2:T(2,128)(2,1)S(1)}, u32[]{:S(2)}, u32[]{:S(2)}) async-start(bf16[1,2,256,1024]{3,1,0,2:T(2,128)(2,1)} %copy.34), calls=%async_computation.2 | async-start | bytes 2097152 | tf_op jit(solution)/shard_map/all_to_all | solution.py:92
  42.6 1.6 reshape.130
  44.2 26.7 %all-to-all-done.2 = bf16[1,2,256,1024]{3,1,0,2:T(2,128)(2,1)S(1)} async-done(((bf16[1,2,256,1024]{3,1,0,2:T(2,128)(2,1)}), bf16[1,2,256,1024]{3,1,0,2:T(2,128)(2,1)S(1)}, u32[]{:S(2)}, u32[]{:S(2)}) %all-to-all-start.2) | async-done | bytes 1048608 | tf_op jit(solution)/shard_map/all_to_all | solution.py:92
  71.2 1.6 copy.47
  72.8 3.8 convolution_convert_fusion
  76.7 2.0 copy.48
  78.7 32.2 %all_to_all.60 = bf16[1,64,8,1024]{3,2,0,1:T(8,128)(2,1)S(1)} all-to-all(bf16[1,64,8,1024]{3,2,0,1:T(8,128)(2,1)S(1)} %bitcast_bitcast_fusion), channel_id=1, replica_groups=mesh['dp'=8,'seq'=32] {'seq'}, dimensions={1} | all-to-all | bytes 2097152 | tf_op jit(solution)/shard_map/all_to_all | solution.py:99
  112.3 2.2 fusion.14
  114.5 2.4 fusion.18
  116.9 3.7 copy.27
  120.6 32.4 %all_to_all.61 = bf16[1,2,256,1024]{3,1,0,2:T(2,128)(2,1)S(1)} all-to-all(bf16[1,2,256,1024]{3,1,0,2:T(2,128)(2,1)} %copy.27), channel_id=1, replica_groups=mesh['dp'=8,'seq'=32] {'seq'}, dimensions={2} | all-to-all | bytes 2097152 | tf_op jit(solution)/shard_map/all_to_all | solution.py:81
  153.4 1.6 copy.45
  155.0 3.2 convolution_convert_fusion.1
  158.2 1.9 copy.46
  160.2 32.4 %all_to_all.62 = bf16[1,64,8,1024]{3,2,0,1:T(8,128)(2,1)S(1)} all-to-all(bf16[1,64,8,1024]{3,2,0,1:T(8,128)(2,1)S(1)} %bitcast_bitcast_fusion.1), channel_id=1, replica_groups=mesh['dp'=8,'seq'=32] {'seq'}, dimensions={1} | all-to-all | bytes 2097152 | tf_op jit(solution)/shard_map/all_to_all | solution.py:88
  193.9 3.2 fusion.13
  198.7 3.0 collective-permute-start.3
  202.6 12.4 %convolution_bitcast_fusion.2 = f32[1024,3072]{0,1:T(8,128)} fusion(bf16[1,512,1024]{2,1,0:T(8,128)(2,1)S(1)} %copy-done, bf16[1,3072]{1,0:T(2,128)(2,1)S(1)} %collective-permute-done.3, bf16[512,1024]{1,0:T(8,128)(2,1)S(1)} %copy-done.6, bf16[512,1024]{1,0:T(8,128)(2,1)S(1)} %get-tuple-element.14, bf16[512,1024]{1,0:T(8,128)(2,1)S(1)} %copy-done.5, ...), kind=kOutput, calls=%fused_computation.14 | convolution fusion | flops 3265265664 | bytes 16826368 | tf_op jit(solution)/shard_map/dot_general | solution.py:114
  215.3 5.5 %maximum_convert_fusion = f32[514,3072]{1,0:T(8,128)} fusion(bf16[1,3072]{1,0:T(2,128)(2,1)S(1)} %collective-permute-done.1, bf16[512,3072]{1,0:T(8,128)(2,1)} %copy-done.4, bf16[1,3072]{1,0:T(2,128)(2,1)S(1)} %collective-permute-done), kind=kLoop, calls=%fused_computation.23 | loop fusion | flops 9474048 | bytes 9474048 | tf_op jit(solution)/shard_map/convert_element_type | solution.py:109
  220.7 152.5 %reduce-scatter.3.cloned.1.call-done = f32[128,3072]{0,1:T(8,128)} async-done(((f32[1024,3072]{0,1:T(8,128)}), f32[128,3072]{0,1:T(8,128)}) %reduce-scatter.3.cloned.1.call-update) | async-done | bytes 1572880 | tf_op jit(solution)/shard_map/reduce_scatter | solution.py:113
  373.3 9.3 %fusion.9 = (f32[3072]{0:T(1024)S(1)}, f32[3072]{0:T(1024)S(1)}, f32[3072]{0:T(1024)S(1)}) fusion(f32[514,3072]{1,0:T(8,128)} %maximum_convert_fusion, bf16[512,1024]{1,0:T(8,128)(2,1)S(1)} %copy-done.6, bf16[512,1024]{1,0:T(8,128)(2,1)S(1)} %copy-done.8, bf16[512,1024]{1,0:T(8,128)(2,1)S(1)} %copy-done.5), kind=kLoop, calls=%fused_computation.18 | loop fusion | flops 18865152 | bytes 22056960 | tf_op jit(solution)/shard_map/reduce_sum | solution.py:110
  382.7 75.7 %psum.7 = f32[3,3072]{1,0:T(4,128)S(1)} all-reduce(f32[3,3072]{1,0:T(4,128)S(1)} %pad_maximum_fusion.9), channel_id=1, replica_groups=mesh['dp'=8,'seq'=32] {'dp','seq'}, use_global_device_ids=true, to_apply=%region_5.6 | all-reduce | flops 9216 | bytes 73728 | tf_op jit(solution)/shard_map/psum | solution.py:111
  459.0 11.0 %fusion.17 = bf16[1,512,1024]{2,1,0:T(8,128)(2,1)} fusion(bf16[1024,3072]{1,0:T(8,128)(2,1)} %param.7, bf16[1,3072]{1,0:T(2,128)(2,1)S(1)} %collective-permute-done.3, bf16[512,1024]{1,0:T(8,128)(2,1)S(1)} %copy-done.6, bf16[512,1024]{1,0:T(8,128)(2,1)} %copy-done.7, bf16[512,1024]{1,0:T(8,128)(2,1)S(1)} %copy-done.5, ...), kind=kOutput, calls=%fused_computation.47 | convolution fusion | flops 3265789952 | bytes 10534912 | tf_op jit(solution)/shard_map/dot_general | solution.py:107
  470.0 22.5 %reduce-scatter.5.cloned.1.call-done = f32[128,96]{0,1:T(8,128)} async-done(((f32[128,3072]{0,1:T(8,128)}), f32[128,96]{0,1:T(8,128)}) %reduce-scatter.5.cloned.1.call-update) | async-done | bytes 49168 | tf_op jit(solution)/shard_map/reduce_scatter | solution.py:119
  492.5 1.4 broadcast_multiply_fusion.1
  (56 shorter events, 9.9 us)
Async XLA Ops:
  7.2 1.2 copy-start
  7.2 11.0 %copy-start.12 = (f32[3,3072]{1,0:T(4,128)S(1)}, f32[3,3072]{1,0:T(4,128)}, u32[]{:S(2)}) copy-start(f32[3,3072]{1,0:T(4,128)} %param.8) | copy-start | bytes 110596
  14.8 12.4 %copy-start.4 = (bf16[512,3072]{1,0:T(8,128)(2,1)}, bf16[512,3072]{1,0:T(8,128)(2,1)S(1)}, u32[]{:S(2)}) copy-start(bf16[512,3072]{1,0:T(8,128)(2,1)S(1)} %convolution_convert_fusion.2) | copy-start | bytes 9437188
  14.8 12.0 %copy-start.9 = (bf16[1,512,1024]{2,1,0:T(8,128)(2,1)S(1)}, bf16[1,512,1024]{2,1,0:T(8,128)(2,1)}, u32[]{:S(2)}) copy-start(bf16[1,512,1024]{2,1,0:T(8,128)(2,1)} %param.6) | copy-start | bytes 3145732
  14.9 3.4 collective-permute-start
  16.9 4.8 collective-permute-start.1
  24.2 2.7 copy-start.2
  26.8 15.7 %copy-start.11 = (bf16[64,8,1024]{2,1,0:T(8,128)(2,1)S(1)}, bf16[64,8,1024]{2,1,0:T(8,128)(2,1)}, u32[]{:S(2)}) copy-start(bf16[64,8,1024]{2,1,0:T(8,128)(2,1)} %param.9) | copy-start | bytes 3145732
  30.7 40.1 %all-to-all-start.2 = ((bf16[1,2,256,1024]{3,1,0,2:T(2,128)(2,1)}), bf16[1,2,256,1024]{3,1,0,2:T(2,128)(2,1)S(1)}, u32[]{:S(2)}, u32[]{:S(2)}) async-start(bf16[1,2,256,1024]{3,1,0,2:T(2,128)(2,1)} %copy.34), calls=%async_computation.2 | async-start | bytes 2097152 | tf_op jit(solution)/shard_map/all_to_all | solution.py:92
  42.5 330.8 %reduce-scatter.3.cloned.1.call-start = ((), (), s32[]{:S(2)}) async-start(), calls=%async_computation.6 | async-start | bytes 14155776 | tf_op jit(solution)/shard_map/reduce_scatter | solution.py:113
  71.2 41.1 %slice-start = ((s8[6291456]{0:T(1024)(128)(4,1)}), s8[2097152]{0:T(1024)(128)(4,1)S(1)}, s32[]{:S(2)}) async-start(s8[6291456]{0:T(1024)(128)(4,1)} %bitcast.146), calls=%async_computation.8 | async-start | bytes 4194304
  76.7 35.6 %slice-start.1 = ((s8[6291456]{0:T(1024)(128)(4,1)}), s8[4194304]{0:T(1024)(128)(4,1)S(1)}, s32[]{:S(2)}) async-start(s8[6291456]{0:T(1024)(128)(4,1)} %bitcast.146), calls=%async_computation.9 | async-start | bytes 8388608
  114.5 40.5 %copy-start.3 = (f32[1,64,8192]{2,1,0:T(8,128)S(1)}, f32[1,64,8192]{2,1,0:T(8,128)}, u32[]{:S(2)}) copy-start(f32[1,64,8192]{2,1,0:T(8,128)} %reshape.130) | copy-start | bytes 6291460
  158.2 35.7 %copy-start.10 = (bf16[1,512,1024]{2,1,0:T(8,128)(2,1)S(1)}, bf16[1,512,1024]{2,1,0:T(8,128)(2,1)}, u32[]{:S(2)}) copy-start(bf16[1,512,1024]{2,1,0:T(8,128)(2,1)} %param.6) | copy-start | bytes 3145732
  160.2 37.0 %copy-start.5 = (bf16[512,1024]{1,0:T(8,128)(2,1)S(1)}, bf16[512,1024]{1,0:T(8,128)(2,1)}, u32[]{:S(2)}) copy-start(bf16[512,1024]{1,0:T(8,128)(2,1)} %get-tuple-element.7) | copy-start | bytes 3145732
  160.2 37.0 %copy-start.6 = (bf16[512,1024]{1,0:T(8,128)(2,1)S(1)}, bf16[512,1024]{1,0:T(8,128)(2,1)}, u32[]{:S(2)}) copy-start(bf16[512,1024]{1,0:T(8,128)(2,1)} %get-tuple-element.8) | copy-start | bytes 3145732
  197.1 5.5 %copy-start.7 = (bf16[512,1024]{1,0:T(8,128)(2,1)}, bf16[512,1024]{1,0:T(8,128)(2,1)S(1)}, u32[]{:S(2)}) copy-start(bf16[512,1024]{1,0:T(8,128)(2,1)S(1)} %get-tuple-element.14) | copy-start | bytes 3145732
  197.4 4.3 collective-permute-start.2
  198.7 3.9 collective-permute-start.3
  215.0 158.3 %copy-start.8 = (bf16[512,1024]{1,0:T(8,128)(2,1)S(1)}, bf16[512,1024]{1,0:T(8,128)(2,1)}, u32[]{:S(2)}) copy-start(bf16[512,1024]{1,0:T(8,128)(2,1)} %copy-done.7) | copy-start | bytes 3145732
  215.0 277.5 %reduce-scatter.5.cloned.1.call-start = ((), (), s32[]{:S(2)}) async-start(), calls=%async_computation.7 | async-start | bytes 1622016 | tf_op jit(solution)/shard_map/reduce_scatter | solution.py:119
  459.0 35.0 %copy-start.1 = (bf16[1,512,1024]{2,1,0:T(8,128)(2,1)S(1)}, bf16[1,512,1024]{2,1,0:T(8,128)(2,1)}, u32[]{:S(2)}) copy-start(bf16[1,512,1024]{2,1,0:T(8,128)(2,1)} %param.5) | copy-start | bytes 3145732
Sparse Core Ops, SparseCore 0:
  215.1 158.0 reduce-scatter.2
  375.9 116.5 reduce-scatter.4
where the time goes:
time: 502 us; the launch traced here: 501 us
  waiting for transfers between devices  206 us (41%)
  blocking collectives  173 us (34%)
  matrix products  43.3 us (9%)
  other arithmetic  25.5 us (5%)
  starting transfers between devices  19.7 us (4%)
  local copies, waits for them, and re-layouts  19.3 us (4%)
  between operations  14.4 us (3%)
    reduce_scatter x1, waiting for transfers between devices, shards(): lax.psum_scatter(lax.dot_general(rows, du, contract, preferred_element_ty...  153 us
    psum x1, blocking collectives, shards(): taps_grad = lax.psum(local_taps, ('dp', 'seq')) * factor  75.7 us
    all_to_all x1, blocking collectives, shards(): lax.all_to_all(block_section(w.reshape(1, nblocks, BLK, width), table_q),...  32.4 us
    all_to_all x1, blocking collectives, shards(): lax.all_to_all(span_section(columns, filt, table_p), 'seq', split_axis=1,...  32.4 us
    all_to_all x1, blocking collectives, shards(): lax.all_to_all(span_section(grad_cols, filt, table_p), 'seq', split_axis=...  32.2 us
    all_to_all x1, waiting for transfers between devices, shards(): lax.all_to_all(block_section(e4.reshape(1, nblocks, BLK, width), table_q)...  26.7 us
    reduce_scatter x1, waiting for transfers between devices, shards(): lax.psum_scatter(partial_sum, 'seq', scatter_dimension=1, tiled=True)  22.5 us
    dot_general x1, matrix products, shards(): lax.dot_general(rows, du, contract, preferred_element_type=jnp.float32)  12.4 us
  transfers between devices with their start and end apart: 7, of which 5 were waited for; matrix products, arithmetic and copies ran while one was open for 6% of the time, Pallas kernels for 0%

commit v1 on v0

--- a/solution.py
+++ b/solution.py
@@ -108,7 +108,7 @@
     dsf = ds.astype(jnp.float32)
     zf = zpad.astype(jnp.float32)
     local_taps = jnp.stack([jnp.sum(dsf * zf[k : k + tok], axis=0) for k in range(3)])
-    taps_grad = lax.psum(local_taps, ("dp", "seq")) * factor
+    taps_grad = lax.psum(lax.psum(local_taps, "dp"), "seq") * factor
     contract = (((0,), (0,)), ((), ()))
     partial_sum = lax.psum_scatter(
         lax.dot_general(rows, du, contract, preferred_element_type=jnp.float32),

time: 502 us -> 547 us (1.090)
  blocking collectives: 173 us -> 239 us
  waiting for transfers between devices: 206 us -> 184 us
    psum x1 -> x2, blocking collectives: 75.7 us -> 142 us  [shards(): taps_grad = lax.psum(lax.psum(local_taps, 'dp'), 'seq') * factor]
    reduce_scatter x1, waiting for transfers between devices: 22.5 us -> 0.01 us  [shards(): lax.psum_scatter(partial_sum, 'seq', scatter_dimension=1, tiled=True)]
  transfers between devices with their start and end apart: 7 -> 7, of which waited for: 5 -> 4; matrix products, arithmetic and copies ran while one was open for 6% -> 5% of each run, Pallas kernels for 0% -> 0%
where the time goes in v1:
time: 547 us; the launch traced here: 545 us
  blocking collectives  239 us (44%)
  waiting for transfers between devices  184 us (34%)
  matrix products  43.2 us (8%)
  other arithmetic  25.5 us (5%)
  starting transfers between devices  19.7 us (4%)
  local copies, waits for them, and re-layouts  19.3 us (4%)
  between operations  14.4 us (3%)
    reduce_scatter x1, waiting for transfers between devices, shards(): lax.psum_scatter(lax.dot_general(rows, du, contract, preferred_element_ty...  153 us
    psum x2, blocking collectives, shards(): taps_grad = lax.psum(lax.psum(local_taps, 'dp'), 'seq') * factor  142 us
    all_to_all x1, blocking collectives, shards(): lax.all_to_all(block_section(w.reshape(1, nblocks, BLK, width), table_q),...  32.5 us
    all_to_all x1, blocking collectives, shards(): lax.all_to_all(span_section(columns, filt, table_p), 'seq', split_axis=1,...  32.4 us
    all_to_all x1, blocking collectives, shards(): lax.all_to_all(span_section(grad_cols, filt, table_p), 'seq', split_axis=...  32.2 us
    all_to_all x1, waiting for transfers between devices, shards(): lax.all_to_all(block_section(e4.reshape(1, nblocks, BLK, width), table_q)...  26.7 us
    dot_general x1, matrix products, shards(): lax.dot_general(rows, du, contract, preferred_element_type=jnp.float32)  12.3 us
    all_to_all x1, starting transfers between devices, shards(): lax.all_to_all(block_section(e4.reshape(1, nblocks, BLK, width), table_q)...  11.8 us
  transfers between devices with their start and end apart: 7, of which 4 were waited for; matrix products, arithmetic and copies ran while one was open for 5% of the time, Pallas kernels for 0%

profile of v1, /device:TPU:2, one launch (start us, length us, event | category | flops | bytes accessed | tf_op | source)
XLA Modules:
  0.0 544.7 jit_solution(9649329210118510357)
XLA Ops:
  8.4 6.4 %convolution_convert_fusion.2 = bf16[512,3072]{1,0:T(8,128)(2,1)S(1)} fusion(bf16[1024,3072]{1,0:T(8,128)(2,1)} %param.7, bf16[1,512,1024]{2,1,0:T(8,128)(2,1)S(1)} %copy-done), kind=kOutput, calls=%fused_computation.22 | convolution fusion | flops 3222798336 | bytes 10485760 | tf_op jit(solution)/shard_map/dot_general | solution.py:72
  14.9 2.0 collective-permute-start
  18.2 3.4 collective-permute-done.1
  21.6 2.5 multiply_add_fusion
  24.2 2.7 copy-done.2
  27.2 1.4 fusion.19
  28.6 2.1 copy.34
  30.7 11.8 %all-to-all-start.2 = ((bf16[1,2,256,1024]{3,1,0,2:T(2,128)(2,1)}), bf16[1,2,256,1024]{3,1,0,2:T(2,128)(2,1)S(1)}, u32[]{:S(2)}, u32[]{:S(2)}) async-start(bf16[1,2,256,1024]{3,1,0,2:T(2,128)(2,1)} %copy.34), calls=%async_computation.2 | async-start | bytes 2097152 | tf_op jit(solution)/shard_map/all_to_all | solution.py:92
  42.6 1.6 reshape.130
  44.1 26.7 %all-to-all-done.2 = bf16[1,2,256,1024]{3,1,0,2:T(2,128)(2,1)S(1)} async-done(((bf16[1,2,256,1024]{3,1,0,2:T(2,128)(2,1)}), bf16[1,2,256,1024]{3,1,0,2:T(2,128)(2,1)S(1)}, u32[]{:S(2)}, u32[]{:S(2)}) %all-to-all-start.2) | async-done | bytes 1048608 | tf_op jit(solution)/shard_map/all_to_all | solution.py:92
  71.2 1.6 copy.47
  72.8 3.8 convolution_convert_fusion
  76.7 2.0 copy.48
  78.7 32.2 %all_to_all.60 = bf16[1,64,8,1024]{3,2,0,1:T(8,128)(2,1)S(1)} all-to-all(bf16[1,64,8,1024]{3,2,0,1:T(8,128)(2,1)S(1)} %bitcast_bitcast_fusion), channel_id=1, replica_groups=mesh['dp'=8,'seq'=32] {'seq'}, dimensions={1} | all-to-all | bytes 2097152 | tf_op jit(solution)/shard_map/all_to_all | solution.py:99
  112.3 2.2 fusion.14
  114.6 2.4 fusion.18
  116.9 3.7 copy.27
  120.7 32.5 %all_to_all.61 = bf16[1,2,256,1024]{3,1,0,2:T(2,128)(2,1)S(1)} all-to-all(bf16[1,2,256,1024]{3,1,0,2:T(2,128)(2,1)} %copy.27), channel_id=1, replica_groups=mesh['dp'=8,'seq'=32] {'seq'}, dimensions={2} | all-to-all | bytes 2097152 | tf_op jit(solution)/shard_map/all_to_all | solution.py:81
  153.5 1.6 copy.45
  155.1 3.2 convolution_convert_fusion.1
  158.2 1.9 copy.46
  160.3 32.4 %all_to_all.62 = bf16[1,64,8,1024]{3,2,0,1:T(8,128)(2,1)S(1)} all-to-all(bf16[1,64,8,1024]{3,2,0,1:T(8,128)(2,1)S(1)} %bitcast_bitcast_fusion.1), channel_id=1, replica_groups=mesh['dp'=8,'seq'=32] {'seq'}, dimensions={1} | all-to-all | bytes 2097152 | tf_op jit(solution)/shard_map/all_to_all | solution.py:88
  194.0 3.2 fusion.13
  198.8 3.0 collective-permute-start.3
  202.7 12.3 %convolution_bitcast_fusion.2 = f32[1024,3072]{0,1:T(8,128)} fusion(bf16[1,512,1024]{2,1,0:T(8,128)(2,1)S(1)} %copy-done, bf16[1,3072]{1,0:T(2,128)(2,1)S(1)} %collective-permute-done.3, bf16[512,1024]{1,0:T(8,128)(2,1)S(1)} %copy-done.6, bf16[512,1024]{1,0:T(8,128)(2,1)S(1)} %get-tuple-element.14, bf16[512,1024]{1,0:T(8,128)(2,1)S(1)} %copy-done.5, ...), kind=kOutput, calls=%fused_computation.14 | convolution fusion | flops 3265265664 | bytes 16826368 | tf_op jit(solution)/shard_map/dot_general | solution.py:114
  215.3 5.5 %maximum_convert_fusion = f32[514,3072]{1,0:T(8,128)} fusion(bf16[1,3072]{1,0:T(2,128)(2,1)S(1)} %collective-permute-done.1, bf16[512,3072]{1,0:T(8,128)(2,1)} %copy-done.4, bf16[1,3072]{1,0:T(2,128)(2,1)S(1)} %collective-permute-done), kind=kLoop, calls=%fused_computation.23 | loop fusion | flops 9474048 | bytes 9474048 | tf_op jit(solution)/shard_map/convert_element_type | solution.py:109
  220.8 152.6 %reduce-scatter.3.cloned.1.call-done = f32[128,3072]{0,1:T(8,128)} async-done(((f32[1024,3072]{0,1:T(8,128)}), f32[128,3072]{0,1:T(8,128)}) %reduce-scatter.3.cloned.1.call-update) | async-done | bytes 1572880 | tf_op jit(solution)/shard_map/reduce_scatter | solution.py:113
  373.4 9.3 %fusion.9 = (f32[3072]{0:T(1024)S(1)}, f32[3072]{0:T(1024)S(1)}, f32[3072]{0:T(1024)S(1)}) fusion(f32[514,3072]{1,0:T(8,128)} %maximum_convert_fusion, bf16[512,1024]{1,0:T(8,128)(2,1)S(1)} %copy-done.6, bf16[512,1024]{1,0:T(8,128)(2,1)S(1)} %copy-done.8, bf16[512,1024]{1,0:T(8,128)(2,1)S(1)} %copy-done.5), kind=kLoop, calls=%fused_computation.18 | loop fusion | flops 18865152 | bytes 22056960 | tf_op jit(solution)/shard_map/reduce_sum | solution.py:110
  382.8 36.9 %psum.14 = f32[3,3072]{1,0:T(4,128)S(1)} all-reduce(f32[3,3072]{1,0:T(4,128)S(1)} %pad_maximum_fusion.9), channel_id=1, replica_groups=mesh['dp'=8,'seq'=32] {'dp'}, use_global_device_ids=true, to_apply=%region_5.6 | all-reduce | flops 9216 | bytes 73728 | tf_op jit(solution)/shard_map/psum | solution.py:111
  419.7 105.1 %psum.15 = f32[3,3072]{1,0:T(4,128)S(1)} all-reduce(f32[3,3072]{1,0:T(4,128)S(1)} %psum.14), channel_id=1, replica_groups=mesh['dp'=8,'seq'=32] {'seq'}, use_global_device_ids=true, to_apply=%region_6.7 | all-reduce | flops 9216 | bytes 73728 | tf_op jit(solution)/shard_map/psum | solution.py:111
  525.4 11.0 %fusion.17 = bf16[1,512,1024]{2,1,0:T(8,128)(2,1)} fusion(bf16[1024,3072]{1,0:T(8,128)(2,1)} %param.7, bf16[1,3072]{1,0:T(2,128)(2,1)S(1)} %collective-permute-done.3, bf16[512,1024]{1,0:T(8,128)(2,1)S(1)} %copy-done.6, bf16[512,1024]{1,0:T(8,128)(2,1)} %copy-done.7, bf16[512,1024]{1,0:T(8,128)(2,1)S(1)} %copy-done.5, ...), kind=kOutput, calls=%fused_computation.47 | convolution fusion | flops 3265789952 | bytes 10534912 | tf_op jit(solution)/shard_map/dot_general | solution.py:107
  536.4 1.4 broadcast_multiply_fusion.1
  (57 shorter events, 9.9 us)
Async XLA Ops:
  7.2 1.2 copy-start
  7.2 11.0 %copy-start.12 = (f32[3,3072]{1,0:T(4,128)S(1)}, f32[3,3072]{1,0:T(4,128)}, u32[]{:S(2)}) copy-start(f32[3,3072]{1,0:T(4,128)} %param.8) | copy-start | bytes 110596
  14.8 12.4 %copy-start.4 = (bf16[512,3072]{1,0:T(8,128)(2,1)}, bf16[512,3072]{1,0:T(8,128)(2,1)S(1)}, u32[]{:S(2)}) copy-start(bf16[512,3072]{1,0:T(8,128)(2,1)S(1)} %convolution_convert_fusion.2) | copy-start | bytes 9437188
  14.8 12.0 %copy-start.9 = (bf16[1,512,1024]{2,1,0:T(8,128)(2,1)S(1)}, bf16[1,512,1024]{2,1,0:T(8,128)(2,1)}, u32[]{:S(2)}) copy-start(bf16[1,512,1024]{2,1,0:T(8,128)(2,1)} %param.6) | copy-start | bytes 3145732
  14.9 3.4 collective-permute-start
  16.9 4.8 collective-permute-start.1
  24.2 2.7 copy-start.2
  26.8 15.7 %copy-start.11 = (bf16[64,8,1024]{2,1,0:T(8,128)(2,1)S(1)}, bf16[64,8,1024]{2,1,0:T(8,128)(2,1)}, u32[]{:S(2)}) copy-start(bf16[64,8,1024]{2,1,0:T(8,128)(2,1)} %param.9) | copy-start | bytes 3145732
  30.7 40.2 %all-to-all-start.2 = ((bf16[1,2,256,1024]{3,1,0,2:T(2,128)(2,1)}), bf16[1,2,256,1024]{3,1,0,2:T(2,128)(2,1)S(1)}, u32[]{:S(2)}, u32[]{:S(2)}) async-start(bf16[1,2,256,1024]{3,1,0,2:T(2,128)(2,1)} %copy.34), calls=%async_computation.2 | async-start | bytes 2097152 | tf_op jit(solution)/shard_map/all_to_all | solution.py:92
  42.5 330.9 %reduce-scatter.3.cloned.1.call-start = ((), (), s32[]{:S(2)}) async-start(), calls=%async_computation.6 | async-start | bytes 14155776 | tf_op jit(solution)/shard_map/reduce_scatter | solution.py:113
  71.2 41.1 %slice-start = ((s8[6291456]{0:T(1024)(128)(4,1)}), s8[2097152]{0:T(1024)(128)(4,1)S(1)}, s32[]{:S(2)}) async-start(s8[6291456]{0:T(1024)(128)(4,1)} %bitcast.146), calls=%async_computation.8 | async-start | bytes 4194304
  76.7 35.7 %slice-start.1 = ((s8[6291456]{0:T(1024)(128)(4,1)}), s8[4194304]{0:T(1024)(128)(4,1)S(1)}, s32[]{:S(2)}) async-start(s8[6291456]{0:T(1024)(128)(4,1)} %bitcast.146), calls=%async_computation.9 | async-start | bytes 8388608
  114.6 40.5 %copy-start.3 = (f32[1,64,8192]{2,1,0:T(8,128)S(1)}, f32[1,64,8192]{2,1,0:T(8,128)}, u32[]{:S(2)}) copy-start(f32[1,64,8192]{2,1,0:T(8,128)} %reshape.130) | copy-start | bytes 6291460
  158.2 35.7 %copy-start.10 = (bf16[1,512,1024]{2,1,0:T(8,128)(2,1)S(1)}, bf16[1,512,1024]{2,1,0:T(8,128)(2,1)}, u32[]{:S(2)}) copy-start(bf16[1,512,1024]{2,1,0:T(8,128)(2,1)} %param.6) | copy-start | bytes 3145732
  160.2 37.0 %copy-start.5 = (bf16[512,1024]{1,0:T(8,128)(2,1)S(1)}, bf16[512,1024]{1,0:T(8,128)(2,1)}, u32[]{:S(2)}) copy-start(bf16[512,1024]{1,0:T(8,128)(2,1)} %get-tuple-element.7) | copy-start | bytes 3145732
  160.2 37.0 %copy-start.6 = (bf16[512,1024]{1,0:T(8,128)(2,1)S(1)}, bf16[512,1024]{1,0:T(8,128)(2,1)}, u32[]{:S(2)}) copy-start(bf16[512,1024]{1,0:T(8,128)(2,1)} %get-tuple-element.8) | copy-start | bytes 3145732
  197.2 5.5 %copy-start.7 = (bf16[512,1024]{1,0:T(8,128)(2,1)}, bf16[512,1024]{1,0:T(8,128)(2,1)S(1)}, u32[]{:S(2)}) copy-start(bf16[512,1024]{1,0:T(8,128)(2,1)S(1)} %get-tuple-element.14) | copy-start | bytes 3145732
  197.5 4.3 collective-permute-start.2
  198.8 3.9 collective-permute-start.3
  215.0 158.3 %copy-start.8 = (bf16[512,1024]{1,0:T(8,128)(2,1)S(1)}, bf16[512,1024]{1,0:T(8,128)(2,1)}, u32[]{:S(2)}) copy-start(bf16[512,1024]{1,0:T(8,128)(2,1)} %copy-done.7) | copy-start | bytes 3145732
  215.0 321.4 %reduce-scatter.5.cloned.1.call-start = ((), (), s32[]{:S(2)}) async-start(), calls=%async_computation.7 | async-start | bytes 1622016 | tf_op jit(solution)/shard_map/reduce_scatter | solution.py:119
  525.4 12.4 %copy-start.1 = (bf16[1,512,1024]{2,1,0:T(8,128)(2,1)S(1)}, bf16[1,512,1024]{2,1,0:T(8,128)(2,1)}, u32[]{:S(2)}) copy-start(bf16[1,512,1024]{2,1,0:T(8,128)(2,1)} %param.5) | copy-start | bytes 3145732
Sparse Core Ops, SparseCore 0:
  215.2 158.1 reduce-scatter.2
  376.0 117.0 reduce-scatter.4
